TPU v7x, 32 devices: a whole 2x2x4 slice. The times are simulated.
32 devices in a mesh: parts: 2 (over y), leaf: 4 (over z), top: 4 (over x, core).
Axes of the slice: x: 2, y: 2, z: 4, core: 2. Of those that a mesh axis runs over, the one named last changes fastest.
Arguments:
- right_side: float32 [8, 2560, 256], P(('parts', 'top'), 'leaf'), parts along dimension 0, may hold values from -6 to 6
- leaf_inverse: bfloat16 [8, 2560, 640], P(('parts', 'top'), 'leaf'), parts along dimension 0, as said below
- left_basis: bfloat16 [2, 8, 2560, 128], P(None, ('parts', 'top'), 'leaf'), parts along dimension 1, may hold values from -0.1875 to 0.1875
- right_basis: bfloat16 [2, 8, 2560, 128], P(None, ('parts', 'top'), 'leaf'), parts along dimension 1, may hold values from -6 to 6
- level_caps: bfloat16 [2, 8, 512, 256], P(None, ('parts', 'top'), 'leaf'), parts along dimension 1, may hold values from -0.375 to 0.375
- top_left: bfloat16 [8, 2560, 128], P(('parts', 'top'), 'leaf'), parts along dimension 0, may hold values from -0.1875 to 0.1875
- top_right: bfloat16 [8, 2560, 128], P(('parts', 'top'), 'leaf'), parts along dimension 0, may hold values from -6 to 6
- top_caps: bfloat16 [1024, 512], P(('parts', 'top')), parts along dimension 0, may hold values from -0.25 to 0.25
Outputs:
- solution: float32 [8, 2560, 256], P(('parts', 'top'), 'leaf'), parts along dimension 0
There are 2 independent parts, one for each index of `parts`. A program takes and returns all parts, laid end to end along the dimension named above; each array names one. Nothing has to cross between parts.
Inputs may be any that keep to these rules, and one draw needn't show every extreme that they name: Each leaf block of leaf_inverse is lower triangular with a positive diagonal.
All inputs are finite; a program needn't handle non-finite values.
Results may differ from a plain program's by a relative error of at most 0.0075.
Values may be sent and summed in bfloat16 or wider, within the bound.
No kernel may reach another device: no remote copies, remote signals or barrier semaphores. Data moves between devices by JAX's collectives and lax.ppermute only.
A program may use at most 64 MiB of HBM per device.

v0:
```python
import math
import jax
import jax.numpy as jnp
from jax import lax
from jax.sharding import PartitionSpec as P


def from_partner(value, axis, distance):
    mask = 2**distance
    pairs = [(source, source ^ mask) for source in range(lax.axis_size(axis))]
    return lax.ppermute(value, axis, pairs)


def project_rows(basis, current):
    return lax.dot_general(
        basis,
        current.astype(jnp.bfloat16),
        (((0,), (0,)), ((), ())),
        preferred_element_type=jnp.float32,
    )


def pair_swaps(partial_value, shift_bits):
    position = lax.axis_index("leaf") >> shift_bits
    for bit_index in range(shift_bits):
        partial_value = partial_value + from_partner(partial_value, "leaf", bit_index)
    sibling_sum = from_partner(partial_value.astype(jnp.bfloat16), "leaf", shift_bits).astype(
        partial_value.dtype
    )
    lower_side = position & 1 == 0
    return jnp.where(
        lower_side,
        jnp.concatenate([partial_value, sibling_sum], 0),
        jnp.concatenate([sibling_sum, partial_value], 0),
    )


def level_update(current, project_basis, update_basis, caps_rows, level_num):
    leaf_rows = current.shape[0]
    shift_bits = level_num - 1
    partial_value = project_rows(project_basis, current) * (
        1.0 / math.sqrt(leaf_rows * 2**shift_bits)
    )
    stacked = pair_swaps(partial_value, shift_bits)
    weights = jnp.dot(
        caps_rows, stacked.astype(jnp.bfloat16), preferred_element_type=jnp.float32
    ).astype(jnp.bfloat16)
    return current - jnp.dot(update_basis, weights, preferred_element_type=jnp.float32)


def top_update(current, project_basis, update_basis, caps_rows):
    leaf_count = lax.axis_size("leaf")
    partial_value = project_rows(project_basis, current) * (
        1.0 / math.sqrt(leaf_count * current.shape[0])
    )
    column_total = lax.psum(partial_value, "leaf")
    stacked = lax.all_gather(column_total.astype(jnp.bfloat16), "top", axis=0, tiled=True)
    weights = jnp.dot(caps_rows, stacked, preferred_element_type=jnp.float32).astype(jnp.bfloat16)
    return current - jnp.dot(update_basis, weights, preferred_element_type=jnp.float32)


def on_device(
    right_side, leaf_inverse, left_basis, right_basis, level_caps, top_left, top_right, top_caps
):
    levels = left_basis.shape[0]
    inverse_block = leaf_inverse[0]
    current = jnp.dot(
        inverse_block, right_side[0].astype(jnp.bfloat16), preferred_element_type=jnp.float32
    )
    for level_num in range(1, levels + 1):
        current = level_update(
            current,
            right_basis[level_num - 1, 0],
            left_basis[level_num - 1, 0],
            level_caps[level_num - 1, 0],
            level_num,
        )
    current = top_update(current, top_right[0], top_left[0], top_caps)
    current = top_update(current, top_left[0], top_right[0], top_caps)
    for level_num in range(levels, 0, -1):
        current = level_update(
            current,
            left_basis[level_num - 1, 0],
            right_basis[level_num - 1, 0],
            level_caps[level_num - 1, 0],
            level_num,
        )
    current = project_rows(inverse_block, current)
    return current[None]


def solution(mesh):
    return jax.shard_map(
        on_device,
        mesh=mesh,
        in_specs=(
            P(("parts", "top"), "leaf", None),
            P(("parts", "top"), "leaf", None),
            P(None, ("parts", "top"), "leaf", None),
            P(None, ("parts", "top"), "leaf", None),
            P(None, ("parts", "top"), "leaf", None),
            P(("parts", "top"), "leaf", None),
            P(("parts", "top"), "leaf", None),
            P(("parts", "top"), None),
        ),
        out_specs=P(("parts", "top"), "leaf", None),
        check_vma=False,
    )
```

profile of v0, /device:TPU:0, one launch (start us, length us, event | category | flops | bytes accessed | tf_op | source)
XLA Modules:
  0.0 93.3 jit_solution(5820424412641615513)
XLA Ops:
  0.0 1.1 %copy-done = bf16[1,640,640]{2,1,0:T(8,128)(2,1)S(1)} copy-done((bf16[1,640,640]{2,1,0:T(8,128)(2,1)S(1)}, bf16[1,640,640]{2,1,0:T(8,128)(2,1)}, u32[]{:S(2)}) %copy-start) | copy-done | bytes 819224
  1.1 1.5 %fusion.14 = f32[640,256]{1,0:T(8,128)S(1)} fusion(bf16[1,640,640]{2,1,0:T(8,128)(2,1)S(1)} %copy-done, f32[1,640,256]{2,1,0:T(8,128)} %param.8), kind=kOutput, calls=%fused_computation.33 | convolution fusion | flops 209879040 | bytes 2129920 | tf_op jit(solution)/shard_map/dot_general | solution.py:67
  2.7 0.3 fusion.12
  3.0 3.1 %collective-permute-start = (bf16[128,256]{1,0:T(8,128)(2,1)S(1)}, bf16[128,256]{1,0:T(8,128)(2,1)S(1)}, u32[]{:S(2)}, u32[]{:S(2)}) collective-permute-start(bf16[128,256]{1,0:T(8,128)(2,1)S(1)} %fusion.12), channel_id=1, source_target_pairs={{0,4},{4,0},{8,12},{12,8},{1,5},{5,1},{9,13},{13,9},{2,6},{6,2},{1... | collective-permute-start | bytes 196616 | tf_op jit(solution)/shard_map/ppermute | solution.py:11
  6.1 2.2 %collective-permute-done = bf16[128,256]{1,0:T(8,128)(2,1)S(1)} collective-permute-done((bf16[128,256]{1,0:T(8,128)(2,1)S(1)}, bf16[128,256]{1,0:T(8,128)(2,1)S(1)}, u32[]{:S(2)}, u32[]{:S(2)}) %collective-permute-start) | collective-permute-done | bytes 65568 | tf_op jit(solution)/shard_map/ppermute | solution.py:11
  8.3 0.5 fusion.5
  8.8 0.3 fusion.11
  9.1 2.1 %collective-permute-start.1 = (f32[128,256]{1,0:T(8,128)S(1)}, f32[128,256]{1,0:T(8,128)S(1)}, u32[]{:S(2)}, u32[]{:S(2)}) collective-permute-start(f32[128,256]{1,0:T(8,128)S(1)} %fusion.11), channel_id=1, source_target_pairs={{0,4},{4,0},{8,12},{12,8},{1,5},{5,1},{9,13},{13,9},{2,6},{6,2},{1... | collective-permute-start | bytes 393224 | tf_op jit(solution)/shard_map/ppermute | solution.py:11
  11.1 3.0 %collective-permute-done.1 = f32[128,256]{1,0:T(8,128)S(1)} collective-permute-done((f32[128,256]{1,0:T(8,128)S(1)}, f32[128,256]{1,0:T(8,128)S(1)}, u32[]{:S(2)}, u32[]{:S(2)}) %collective-permute-start.1) | collective-permute-done | bytes 131104 | tf_op jit(solution)/shard_map/ppermute | solution.py:11
  14.1 3.1 %collective-permute-start.2 = (bf16[128,256]{1,0:T(8,128)(2,1)S(1)}, bf16[128,256]{1,0:T(8,128)(2,1)S(1)}, u32[]{:S(2)}, u32[]{:S(2)}) collective-permute-start(bf16[128,256]{1,0:T(8,128)(2,1)S(1)} %add.10), channel_id=1, source_target_pairs={{0,8},{4,12},{8,0},{12,4},{1,9},{5,13},{9,1},{13,5},{2,10},{6,14},... | collective-permute-start | bytes 196616 | tf_op jit(solution)/shard_map/ppermute | solution.py:11
  17.2 2.2 %collective-permute-done.2 = bf16[128,256]{1,0:T(8,128)(2,1)S(1)} collective-permute-done((bf16[128,256]{1,0:T(8,128)(2,1)S(1)}, bf16[128,256]{1,0:T(8,128)(2,1)S(1)}, u32[]{:S(2)}, u32[]{:S(2)}) %collective-permute-start.2) | collective-permute-done | bytes 65568 | tf_op jit(solution)/shard_map/ppermute | solution.py:11
  19.5 0.5 fusion.4
  20.0 0.3 fusion.10
  20.3 22.1 %all-reduce.2 = bf16[128,256]{0,1:T(8,128)(2,1)S(1)} all-reduce(f32[128,256]{0,1:T(8,128)S(1)} %fusion.10), channel_id=1, replica_groups=mesh['parts'=2,'leaf'=4,'top'=4] {'leaf'}, use_global_device_ids=true, to_apply=%region_0.1 | all-reduce | flops 32768 | bytes 196608 | tf_op jit(solution)/shard_map/psum | solution.py:56
  42.4 5.9 %all_gather.6 = bf16[512,256]{0,1:T(8,128)(2,1)S(1)} all-gather(bf16[128,256]{0,1:T(8,128)(2,1)S(1)} %all-reduce.2), channel_id=1, replica_groups=mesh['parts'=2,'leaf'=4,'top'=4] {'top'}, dimensions={0}, use_global_device_ids=true | all-gather | bytes 327680 | tf_op jit(solution)/shard_map/all_gather | solution.py:57
  48.3 0.6 fusion.3
  48.9 0.3 fusion.9
  49.2 18.4 %all-reduce.3 = bf16[128,256]{0,1:T(8,128)(2,1)S(1)} all-reduce(f32[128,256]{0,1:T(8,128)S(1)} %fusion.9), channel_id=1, replica_groups=mesh['parts'=2,'leaf'=4,'top'=4] {'leaf'}, use_global_device_ids=true, to_apply=%region_1.2 | all-reduce | flops 32768 | bytes 196608 | tf_op jit(solution)/shard_map/psum | solution.py:56
  67.7 5.9 %all_gather.7 = bf16[512,256]{0,1:T(8,128)(2,1)S(1)} all-gather(bf16[128,256]{0,1:T(8,128)(2,1)S(1)} %all-reduce.3), channel_id=1, replica_groups=mesh['parts'=2,'leaf'=4,'top'=4] {'top'}, dimensions={0}, use_global_device_ids=true | all-gather | bytes 327680 | tf_op jit(solution)/shard_map/all_gather | solution.py:57
  73.6 0.6 fusion.2
  74.2 0.3 fusion.8
  74.5 0.1 collective-permute-start.3
  74.6 5.7 %collective-permute-done.3 = f32[128,256]{1,0:T(8,128)S(1)} collective-permute-done((f32[128,256]{1,0:T(8,128)S(1)}, f32[128,256]{1,0:T(8,128)S(1)}, u32[]{:S(2)}, u32[]{:S(2)}) %collective-permute-start.3) | collective-permute-done | bytes 131104 | tf_op jit(solution)/shard_map/ppermute | solution.py:11
  80.3 0.8 collective-permute-start.4
  81.1 5.1 %collective-permute-done.4 = bf16[128,256]{1,0:T(8,128)(2,1)S(1)} collective-permute-done((bf16[128,256]{1,0:T(8,128)(2,1)S(1)}, bf16[128,256]{1,0:T(8,128)(2,1)S(1)}, u32[]{:S(2)}, u32[]{:S(2)}) %collective-permute-start.4) | collective-permute-done | bytes 65568 | tf_op jit(solution)/shard_map/ppermute | solution.py:11
  86.2 0.5 fusion.1
  86.7 0.3 fusion.7
  86.9 0.1 collective-permute-start.5
  87.0 4.3 %collective-permute-done.5 = bf16[128,256]{1,0:T(8,128)(2,1)S(1)} collective-permute-done((bf16[128,256]{1,0:T(8,128)(2,1)S(1)}, bf16[128,256]{1,0:T(8,128)(2,1)S(1)}, u32[]{:S(2)}, u32[]{:S(2)}) %collective-permute-start.5) | collective-permute-done | bytes 65568 | tf_op jit(solution)/shard_map/ppermute | solution.py:11
  91.3 0.2 convolution_convert_fusion.2
  91.5 0.8 convolution_bitcast_fusion
  92.3 1.1 %copy.14 = f32[1,640,256]{2,1,0:T(8,128)} copy(f32[1,640,256]{1,2,0:T(8,128)S(1)} %convolution_bitcast_fusion) | data formatting | bytes 1310720 | tf_op jit(solution)/shard_map/broadcast_in_dim | solution.py:89
  (21 shorter events, 0.1 us)
Async XLA Ops:
  0.0 1.1 %copy-start = (bf16[1,640,640]{2,1,0:T(8,128)(2,1)S(1)}, bf16[1,640,640]{2,1,0:T(8,128)(2,1)}, u32[]{:S(2)}) copy-start(bf16[1,640,640]{2,1,0:T(8,128)(2,1)} %param.9) | copy-start | bytes 2457604
  0.0 2.7 %copy-start.1 = (bf16[2,1,640,128]{3,2,1,0:T(8,128)(2,1)S(1)}, bf16[2,1,640,128]{3,2,1,0:T(8,128)(2,1)}, u32[]{:S(2)}) copy-start(bf16[2,1,640,128]{3,2,1,0:T(8,128)(2,1)} %param.11) | copy-start | bytes 983044
  2.7 5.6 %copy-start.2 = (bf16[2,1,640,128]{3,2,1,0:T(8,128)(2,1)S(1)}, bf16[2,1,640,128]{3,2,1,0:T(8,128)(2,1)}, u32[]{:S(2)}) copy-start(bf16[2,1,640,128]{3,2,1,0:T(8,128)(2,1)} %param.10) | copy-start | bytes 983044
  2.7 5.6 %copy-start.8 = (bf16[2,1,128,256]{3,2,1,0:T(8,128)(2,1)S(1)}, bf16[2,1,128,256]{3,2,1,0:T(8,128)(2,1)}, u32[]{:S(2)}) copy-start(bf16[2,1,128,256]{3,2,1,0:T(8,128)(2,1)} %param.12) | copy-start | bytes 393220
  3.0 5.3 %collective-permute-start = (bf16[128,256]{1,0:T(8,128)(2,1)S(1)}, bf16[128,256]{1,0:T(8,128)(2,1)S(1)}, u32[]{:S(2)}, u32[]{:S(2)}) collective-permute-start(bf16[128,256]{1,0:T(8,128)(2,1)S(1)} %fusion.12), channel_id=1, source_target_pairs={{0,4},{4,0},{8,12},{12,8},{1,5},{5,1},{9,13},{13,9},{2,6},{6,2},{1... | collective-permute-start | bytes 196616 | tf_op jit(solution)/shard_map/ppermute | solution.py:11
  9.1 5.0 %collective-permute-start.1 = (f32[128,256]{1,0:T(8,128)S(1)}, f32[128,256]{1,0:T(8,128)S(1)}, u32[]{:S(2)}, u32[]{:S(2)}) collective-permute-start(f32[128,256]{1,0:T(8,128)S(1)} %fusion.11), channel_id=1, source_target_pairs={{0,4},{4,0},{8,12},{12,8},{1,5},{5,1},{9,13},{13,9},{2,6},{6,2},{1... | collective-permute-start | bytes 393224 | tf_op jit(solution)/shard_map/ppermute | solution.py:11
  14.1 5.3 %collective-permute-start.2 = (bf16[128,256]{1,0:T(8,128)(2,1)S(1)}, bf16[128,256]{1,0:T(8,128)(2,1)S(1)}, u32[]{:S(2)}, u32[]{:S(2)}) collective-permute-start(bf16[128,256]{1,0:T(8,128)(2,1)S(1)} %add.10), channel_id=1, source_target_pairs={{0,8},{4,12},{8,0},{12,4},{1,9},{5,13},{9,1},{13,5},{2,10},{6,14},... | collective-permute-start | bytes 196616 | tf_op jit(solution)/shard_map/ppermute | solution.py:11
  17.2 2.7 %copy-start.4 = (bf16[1,640,128]{2,1,0:T(8,128)(2,1)S(1)}, bf16[1,640,128]{2,1,0:T(8,128)(2,1)}, u32[]{:S(2)}) copy-start(bf16[1,640,128]{2,1,0:T(8,128)(2,1)} %param.14) | copy-start | bytes 491524
  42.4 6.0 %copy-start.3 = (bf16[1,640,128]{2,1,0:T(8,128)(2,1)S(1)}, bf16[1,640,128]{2,1,0:T(8,128)(2,1)}, u32[]{:S(2)}) copy-start(bf16[1,640,128]{2,1,0:T(8,128)(2,1)} %param.13) | copy-start | bytes 491524
  42.4 6.0 %copy-start.6 = (bf16[128,512]{1,0:T(8,128)(2,1)S(1)}, bf16[128,512]{1,0:T(8,128)(2,1)}, u32[]{:S(2)}) copy-start(bf16[128,512]{1,0:T(8,128)(2,1)} %param.15) | copy-start | bytes 393220
  67.7 6.0 %copy-start.5 = (bf16[1,640,128]{2,1,0:T(8,128)(2,1)S(1)}, bf16[1,640,128]{2,1,0:T(8,128)(2,1)}, u32[]{:S(2)}) copy-start(bf16[1,640,128]{2,1,0:T(8,128)(2,1)} %param.14) | copy-start | bytes 491524
  67.7 6.0 %copy-start.7 = (bf16[128,512]{1,0:T(8,128)(2,1)S(1)}, bf16[128,512]{1,0:T(8,128)(2,1)}, u32[]{:S(2)}) copy-start(bf16[128,512]{1,0:T(8,128)(2,1)} %param.15) | copy-start | bytes 393220
  74.5 11.7 %copy-start.9 = (bf16[2,1,128,256]{3,2,1,0:T(8,128)(2,1)S(1)}, bf16[2,1,128,256]{3,2,1,0:T(8,128)(2,1)}, u32[]{:S(2)}) copy-start(bf16[2,1,128,256]{3,2,1,0:T(8,128)(2,1)} %param.12) | copy-start | bytes 393220
  74.5 5.8 %collective-permute-start.3 = (f32[128,256]{1,0:T(8,128)S(1)}, f32[128,256]{1,0:T(8,128)S(1)}, u32[]{:S(2)}, u32[]{:S(2)}) collective-permute-start(f32[128,256]{1,0:T(8,128)S(1)} %fusion.8), channel_id=1, source_target_pairs={{0,4},{4,0},{8,12},{12,8},{1,5},{5,1},{9,13},{13,9},{2,6},{6,2},{1... | collective-permute-start | bytes 393224 | tf_op jit(solution)/shard_map/ppermute | solution.py:11
  80.3 5.9 %collective-permute-start.4 = (bf16[128,256]{1,0:T(8,128)(2,1)S(1)}, bf16[128,256]{1,0:T(8,128)(2,1)S(1)}, u32[]{:S(2)}, u32[]{:S(2)}) collective-permute-start(bf16[128,256]{1,0:T(8,128)(2,1)S(1)} %add.11), channel_id=1, source_target_pairs={{0,8},{4,12},{8,0},{12,4},{1,9},{5,13},{9,1},{13,5},{2,10},{6,14},... | collective-permute-start | bytes 196616 | tf_op jit(solution)/shard_map/ppermute | solution.py:11
  86.9 4.3 %collective-permute-start.5 = (bf16[128,256]{1,0:T(8,128)(2,1)S(1)}, bf16[128,256]{1,0:T(8,128)(2,1)S(1)}, u32[]{:S(2)}, u32[]{:S(2)}) collective-permute-start(bf16[128,256]{1,0:T(8,128)(2,1)S(1)} %fusion.7), channel_id=1, source_target_pairs={{0,4},{4,0},{8,12},{12,8},{1,5},{5,1},{9,13},{13,9},{2,6},{6,2},{1... | collective-permute-start | bytes 196616 | tf_op jit(solution)/shard_map/ppermute | solution.py:11
where the time goes:
time: 93.6 us; the launch traced here: 93.3 us
  blocking collectives  52.4 us (56%)
  waiting for transfers between devices  22.5 us (24%)
  starting transfers between devices  9.21 us (10%)
  matrix products  6.72 us (7%)
  local copies, waits for them, and re-layouts  2.27 us (2%)
    psum x2, blocking collectives, top_update(): column_total = lax.psum(partial_value, 'leaf')  40.5 us
    ppermute x6, waiting for transfers between devices, from_partner(): return lax.ppermute(value, axis, pairs)  22.5 us
    all_gather x2, blocking collectives, top_update(): lax.all_gather(column_total.astype(jnp.bfloat16), 'top', axis=0, tiled=True)  11.9 us
    ppermute x6, starting transfers between devices, from_partner(): return lax.ppermute(value, axis, pairs)  9.21 us
    dot_general x7, matrix products, project_rows(): lax.dot_general(basis, current.astype(jnp.bfloat16), (((0,), (0,)), ((),...  2.41 us
  transfers between devices with their start and end apart: 6, of which 6 were waited for; matrix products, arithmetic and copies ran while one was open for 0% of the time, Pallas kernels for 0%

commit v1 on v0

--- a/solution.py
+++ b/solution.py
@@ -53,7 +53,7 @@
     partial_value = project_rows(project_basis, current) * (
         1.0 / math.sqrt(leaf_count * current.shape[0])
     )
-    column_total = lax.psum(partial_value, "leaf")
+    column_total = jnp.sum(lax.all_gather(partial_value, "leaf"), axis=0)
     stacked = lax.all_gather(column_total.astype(jnp.bfloat16), "top", axis=0, tiled=True)
     weights = jnp.dot(caps_rows, stacked, preferred_element_type=jnp.float32).astype(jnp.bfloat16)
     return current - jnp.dot(update_basis, weights, preferred_element_type=jnp.float32)

time: 93.6 us -> 86.1 us (0.920)
  blocking collectives: 52.4 us -> 44.4 us
  waiting for transfers between devices: 22.5 us -> 17.8 us
  starting transfers between devices: 9.21 us -> 13.5 us
    psum x2 -> x0, blocking collectives: 40.5 us -> none  [top_update(): column_total = lax.psum(partial_value, 'leaf')]
    all_gather x0 -> x2, blocking collectives: none -> 32.5 us  [top_update(): column_total = jnp.sum(lax.all_gather(partial_value, 'leaf'), axis=0)]
    ppermute x6, waiting for transfers between devices: 22.5 us -> 17.8 us  [from_partner(): return lax.ppermute(value, axis, pairs)]
    ppermute x6, starting transfers between devices: 9.21 us -> 13.5 us  [from_partner(): return lax.ppermute(value, axis, pairs)]
where the time goes in v1:
time: 86.1 us; the launch traced here: 85.9 us
  blocking collectives  44.4 us (52%)
  waiting for transfers between devices  17.8 us (21%)
  starting transfers between devices  13.5 us (16%)
  matrix products  6.7 us (8%)
  local copies, waits for them, and re-layouts  2.63 us (3%)
    all_gather x2, blocking collectives, top_update(): column_total = jnp.sum(lax.all_gather(partial_value, 'leaf'), axis=0)  32.5 us
    ppermute x6, waiting for transfers between devices, from_partner(): return lax.ppermute(value, axis, pairs)  17.8 us
    ppermute x6, starting transfers between devices, from_partner(): return lax.ppermute(value, axis, pairs)  13.5 us
    all_gather x2, blocking collectives, top_update(): lax.all_gather(column_total.astype(jnp.bfloat16), 'top', axis=0, tiled=True)  11.9 us
    dot_general x7, matrix products, project_rows(): lax.dot_general(basis, current.astype(jnp.bfloat16), (((0,), (0,)), ((),...  2.39 us
  transfers between devices with their start and end apart: 6, of which 6 were waited for; matrix products, arithmetic and copies ran while one was open for 0% of the time, Pallas kernels for 0%

profile of v1, /device:TPU:0, one launch (start us, length us, event | category | flops | bytes accessed | tf_op | source)
XLA Modules:
  0.0 85.9 jit_solution(6157185643568716368)
XLA Ops:
  0.0 1.1 %copy-done = bf16[1,640,640]{2,1,0:T(8,128)(2,1)S(1)} copy-done((bf16[1,640,640]{2,1,0:T(8,128)(2,1)S(1)}, bf16[1,640,640]{2,1,0:T(8,128)(2,1)}, u32[]{:S(2)}) %copy-start) | copy-done | bytes 819224
  1.1 1.5 %fusion.14 = f32[640,256]{1,0:T(8,128)S(1)} fusion(bf16[1,640,640]{2,1,0:T(8,128)(2,1)S(1)} %copy-done, f32[1,640,256]{2,1,0:T(8,128)} %param.8), kind=kOutput, calls=%fused_computation.33 | convolution fusion | flops 209879040 | bytes 2129920 | tf_op jit(solution)/shard_map/dot_general | solution.py:67
  2.7 0.3 fusion.12
  3.0 3.1 %collective-permute-start = (bf16[128,256]{1,0:T(8,128)(2,1)S(1)}, bf16[128,256]{1,0:T(8,128)(2,1)S(1)}, u32[]{:S(2)}, u32[]{:S(2)}) collective-permute-start(bf16[128,256]{1,0:T(8,128)(2,1)S(1)} %fusion.12), channel_id=1, source_target_pairs={{0,4},{4,0},{8,12},{12,8},{1,5},{5,1},{9,13},{13,9},{2,6},{6,2},{1... | collective-permute-start | bytes 196616 | tf_op jit(solution)/shard_map/ppermute | solution.py:11
  6.1 2.2 %collective-permute-done = bf16[128,256]{1,0:T(8,128)(2,1)S(1)} collective-permute-done((bf16[128,256]{1,0:T(8,128)(2,1)S(1)}, bf16[128,256]{1,0:T(8,128)(2,1)S(1)}, u32[]{:S(2)}, u32[]{:S(2)}) %collective-permute-start) | collective-permute-done | bytes 65568 | tf_op jit(solution)/shard_map/ppermute | solution.py:11
  8.3 0.5 fusion.5
  9.1 2.1 %collective-permute-start.1 = (f32[128,256]{1,0:T(8,128)S(1)}, f32[128,256]{1,0:T(8,128)S(1)}, u32[]{:S(2)}, u32[]{:S(2)}) collective-permute-start(f32[128,256]{1,0:T(8,128)S(1)} %fusion.11), channel_id=1, source_target_pairs={{0,4},{4,0},{8,12},{12,8},{1,5},{5,1},{9,13},{13,9},{2,6},{6,2},{1... | collective-permute-start | bytes 393224 | tf_op jit(solution)/shard_map/ppermute | solution.py:11
  11.1 3.0 %collective-permute-done.1 = f32[128,256]{1,0:T(8,128)S(1)} collective-permute-done((f32[128,256]{1,0:T(8,128)S(1)}, f32[128,256]{1,0:T(8,128)S(1)}, u32[]{:S(2)}, u32[]{:S(2)}) %collective-permute-start.1) | collective-permute-done | bytes 131104 | tf_op jit(solution)/shard_map/ppermute | solution.py:11
  14.1 3.1 %collective-permute-start.2 = (bf16[128,256]{1,0:T(8,128)(2,1)S(1)}, bf16[128,256]{1,0:T(8,128)(2,1)S(1)}, u32[]{:S(2)}, u32[]{:S(2)}) collective-permute-start(bf16[128,256]{1,0:T(8,128)(2,1)S(1)} %add.6), channel_id=1, source_target_pairs={{0,8},{4,12},{8,0},{12,4},{1,9},{5,13},{9,1},{13,5},{2,10},{6,14},... | collective-permute-start | bytes 196616 | tf_op jit(solution)/shard_map/ppermute | solution.py:11
  17.2 2.2 %collective-permute-done.2 = bf16[128,256]{1,0:T(8,128)(2,1)S(1)} collective-permute-done((bf16[128,256]{1,0:T(8,128)(2,1)S(1)}, bf16[128,256]{1,0:T(8,128)(2,1)S(1)}, u32[]{:S(2)}, u32[]{:S(2)}) %collective-permute-start.2) | collective-permute-done | bytes 65568 | tf_op jit(solution)/shard_map/ppermute | solution.py:11
  19.5 0.5 fusion.4
  20.0 0.3 fusion.10
  20.3 16.9 %all-gather = f32[512,256]{0,1:T(8,128)S(1)} all-gather(f32[128,256]{0,1:T(8,128)S(1)} %fusion.10), channel_id=2, replica_groups=mesh['parts'=2,'leaf'=4,'top'=4] {'leaf'}, dimensions={0}, use_global_device_ids=true | all-gather | bytes 655360 | tf_op jit(solution)/shard_map/all_gather | solution.py:56
  37.4 0.3 reduce_sum.18
  37.7 5.9 %all_gather.20 = bf16[512,256]{0,1:T(8,128)(2,1)S(1)} all-gather(bf16[128,256]{0,1:T(8,128)(2,1)S(1)} %reduce_sum.18), channel_id=1, replica_groups=mesh['parts'=2,'leaf'=4,'top'=4] {'top'}, dimensions={0}, use_global_device_ids=true | all-gather | bytes 327680 | tf_op jit(solution)/shard_map/all_gather | solution.py:57
  43.7 0.6 fusion.3
  44.2 0.3 fusion.9
  44.5 15.6 %all-gather.1 = f32[512,256]{0,1:T(8,128)S(1)} all-gather(f32[128,256]{0,1:T(8,128)S(1)} %fusion.9), channel_id=3, replica_groups=mesh['parts'=2,'leaf'=4,'top'=4] {'leaf'}, dimensions={0}, use_global_device_ids=true | all-gather | bytes 655360 | tf_op jit(solution)/shard_map/all_gather | solution.py:56
  60.3 0.3 reduce_sum.19
  60.7 5.9 %all_gather.23 = bf16[512,256]{0,1:T(8,128)(2,1)S(1)} all-gather(bf16[128,256]{0,1:T(8,128)(2,1)S(1)} %reduce_sum.19), channel_id=1, replica_groups=mesh['parts'=2,'leaf'=4,'top'=4] {'top'}, dimensions={0}, use_global_device_ids=true | all-gather | bytes 327680 | tf_op jit(solution)/shard_map/all_gather | solution.py:57
  66.6 0.6 fusion.2
  67.2 0.3 fusion.8
  67.5 1.5 %collective-permute-start.3 = (f32[128,256]{1,0:T(8,128)S(1)}, f32[128,256]{1,0:T(8,128)S(1)}, u32[]{:S(2)}, u32[]{:S(2)}) collective-permute-start(f32[128,256]{1,0:T(8,128)S(1)} %fusion.8), channel_id=1, source_target_pairs={{0,4},{4,0},{8,12},{12,8},{1,5},{5,1},{9,13},{13,9},{2,6},{6,2},{1... | collective-permute-start | bytes 393224 | tf_op jit(solution)/shard_map/ppermute | solution.py:11
  69.0 4.3 %collective-permute-done.3 = f32[128,256]{1,0:T(8,128)S(1)} collective-permute-done((f32[128,256]{1,0:T(8,128)S(1)}, f32[128,256]{1,0:T(8,128)S(1)}, u32[]{:S(2)}, u32[]{:S(2)}) %collective-permute-start.3) | collective-permute-done | bytes 131104 | tf_op jit(solution)/shard_map/ppermute | solution.py:11
  73.3 2.3 %collective-permute-start.4 = (bf16[128,256]{1,0:T(8,128)(2,1)S(1)}, bf16[128,256]{1,0:T(8,128)(2,1)S(1)}, u32[]{:S(2)}, u32[]{:S(2)}) collective-permute-start(bf16[128,256]{1,0:T(8,128)(2,1)S(1)} %add.7), channel_id=1, source_target_pairs={{0,8},{4,12},{8,0},{12,4},{1,9},{5,13},{9,1},{13,5},{2,10},{6,14},... | collective-permute-start | bytes 196616 | tf_op jit(solution)/shard_map/ppermute | solution.py:11
  75.6 3.1 %collective-permute-done.4 = bf16[128,256]{1,0:T(8,128)(2,1)S(1)} collective-permute-done((bf16[128,256]{1,0:T(8,128)(2,1)S(1)}, bf16[128,256]{1,0:T(8,128)(2,1)S(1)}, u32[]{:S(2)}, u32[]{:S(2)}) %collective-permute-start.4) | collective-permute-done | bytes 65568 | tf_op jit(solution)/shard_map/ppermute | solution.py:11
  78.7 0.5 fusion.1
  79.2 0.3 fusion.7
  79.5 1.3 %collective-permute-start.5 = (bf16[128,256]{1,0:T(8,128)(2,1)S(1)}, bf16[128,256]{1,0:T(8,128)(2,1)S(1)}, u32[]{:S(2)}, u32[]{:S(2)}) collective-permute-start(bf16[128,256]{1,0:T(8,128)(2,1)S(1)} %fusion.7), channel_id=1, source_target_pairs={{0,4},{4,0},{8,12},{12,8},{1,5},{5,1},{9,13},{13,9},{2,6},{6,2},{1... | collective-permute-start | bytes 196616 | tf_op jit(solution)/shard_map/ppermute | solution.py:11
  80.8 3.0 %collective-permute-done.5 = bf16[128,256]{1,0:T(8,128)(2,1)S(1)} collective-permute-done((bf16[128,256]{1,0:T(8,128)(2,1)S(1)}, bf16[128,256]{1,0:T(8,128)(2,1)S(1)}, u32[]{:S(2)}, u32[]{:S(2)}) %collective-permute-start.5) | collective-permute-done | bytes 65568 | tf_op jit(solution)/shard_map/ppermute | solution.py:11
  84.1 0.7 convolution_bitcast_fusion
  84.8 1.1 %copy.20 = f32[1,640,256]{2,1,0:T(8,128)} copy(f32[1,640,256]{1,2,0:T(8,128)S(1)} %convolution_bitcast_fusion) | data formatting | bytes 1310720 | tf_op jit(solution)/shard_map/broadcast_in_dim | solution.py:89
  (25 shorter events, 0.9 us)
Async XLA Ops:
  0.0 1.1 %copy-start = (bf16[1,640,640]{2,1,0:T(8,128)(2,1)S(1)}, bf16[1,640,640]{2,1,0:T(8,128)(2,1)}, u32[]{:S(2)}) copy-start(bf16[1,640,640]{2,1,0:T(8,128)(2,1)} %param.9) | copy-start | bytes 2457604
  0.0 2.7 %copy-start.1 = (bf16[2,1,640,128]{3,2,1,0:T(8,128)(2,1)S(1)}, bf16[2,1,640,128]{3,2,1,0:T(8,128)(2,1)}, u32[]{:S(2)}) copy-start(bf16[2,1,640,128]{3,2,1,0:T(8,128)(2,1)} %param.11) | copy-start | bytes 983044
  2.7 5.6 %copy-start.2 = (bf16[2,1,640,128]{3,2,1,0:T(8,128)(2,1)S(1)}, bf16[2,1,640,128]{3,2,1,0:T(8,128)(2,1)}, u32[]{:S(2)}) copy-start(bf16[2,1,640,128]{3,2,1,0:T(8,128)(2,1)} %param.10) | copy-start | bytes 983044
  2.7 5.6 %copy-start.8 = (bf16[2,1,128,256]{3,2,1,0:T(8,128)(2,1)S(1)}, bf16[2,1,128,256]{3,2,1,0:T(8,128)(2,1)}, u32[]{:S(2)}) copy-start(bf16[2,1,128,256]{3,2,1,0:T(8,128)(2,1)} %param.12) | copy-start | bytes 393220
  3.0 5.3 %collective-permute-start = (bf16[128,256]{1,0:T(8,128)(2,1)S(1)}, bf16[128,256]{1,0:T(8,128)(2,1)S(1)}, u32[]{:S(2)}, u32[]{:S(2)}) collective-permute-start(bf16[128,256]{1,0:T(8,128)(2,1)S(1)} %fusion.12), channel_id=1, source_target_pairs={{0,4},{4,0},{8,12},{12,8},{1,5},{5,1},{9,13},{13,9},{2,6},{6,2},{1... | collective-permute-start | bytes 196616 | tf_op jit(solution)/shard_map/ppermute | solution.py:11
  9.1 5.0 %collective-permute-start.1 = (f32[128,256]{1,0:T(8,128)S(1)}, f32[128,256]{1,0:T(8,128)S(1)}, u32[]{:S(2)}, u32[]{:S(2)}) collective-permute-start(f32[128,256]{1,0:T(8,128)S(1)} %fusion.11), channel_id=1, source_target_pairs={{0,4},{4,0},{8,12},{12,8},{1,5},{5,1},{9,13},{13,9},{2,6},{6,2},{1... | collective-permute-start | bytes 393224 | tf_op jit(solution)/shard_map/ppermute | solution.py:11
  14.1 5.3 %collective-permute-start.2 = (bf16[128,256]{1,0:T(8,128)(2,1)S(1)}, bf16[128,256]{1,0:T(8,128)(2,1)S(1)}, u32[]{:S(2)}, u32[]{:S(2)}) collective-permute-start(bf16[128,256]{1,0:T(8,128)(2,1)S(1)} %add.6), channel_id=1, source_target_pairs={{0,8},{4,12},{8,0},{12,4},{1,9},{5,13},{9,1},{13,5},{2,10},{6,14},... | collective-permute-start | bytes 196616 | tf_op jit(solution)/shard_map/ppermute | solution.py:11
  17.2 2.7 %copy-start.4 = (bf16[1,640,128]{2,1,0:T(8,128)(2,1)S(1)}, bf16[1,640,128]{2,1,0:T(8,128)(2,1)}, u32[]{:S(2)}) copy-start(bf16[1,640,128]{2,1,0:T(8,128)(2,1)} %param.14) | copy-start | bytes 491524
  37.7 6.0 %copy-start.3 = (bf16[1,640,128]{2,1,0:T(8,128)(2,1)S(1)}, bf16[1,640,128]{2,1,0:T(8,128)(2,1)}, u32[]{:S(2)}) copy-start(bf16[1,640,128]{2,1,0:T(8,128)(2,1)} %param.13) | copy-start | bytes 491524
  37.7 6.0 %copy-start.6 = (bf16[128,512]{1,0:T(8,128)(2,1)S(1)}, bf16[128,512]{1,0:T(8,128)(2,1)}, u32[]{:S(2)}) copy-start(bf16[128,512]{1,0:T(8,128)(2,1)} %param.15) | copy-start | bytes 393220
  60.7 6.0 %copy-start.5 = (bf16[1,640,128]{2,1,0:T(8,128)(2,1)S(1)}, bf16[1,640,128]{2,1,0:T(8,128)(2,1)}, u32[]{:S(2)}) copy-start(bf16[1,640,128]{2,1,0:T(8,128)(2,1)} %param.14) | copy-start | bytes 491524
  60.7 6.0 %copy-start.7 = (bf16[128,512]{1,0:T(8,128)(2,1)S(1)}, bf16[128,512]{1,0:T(8,128)(2,1)}, u32[]{:S(2)}) copy-start(bf16[128,512]{1,0:T(8,128)(2,1)} %param.15) | copy-start | bytes 393220
  67.5 11.3 %copy-start.9 = (bf16[2,1,128,256]{3,2,1,0:T(8,128)(2,1)S(1)}, bf16[2,1,128,256]{3,2,1,0:T(8,128)(2,1)}, u32[]{:S(2)}) copy-start(bf16[2,1,128,256]{3,2,1,0:T(8,128)(2,1)} %param.12) | copy-start | bytes 393220
  67.5 5.8 %collective-permute-start.3 = (f32[128,256]{1,0:T(8,128)S(1)}, f32[128,256]{1,0:T(8,128)S(1)}, u32[]{:S(2)}, u32[]{:S(2)}) collective-permute-start(f32[128,256]{1,0:T(8,128)S(1)} %fusion.8), channel_id=1, source_target_pairs={{0,4},{4,0},{8,12},{12,8},{1,5},{5,1},{9,13},{13,9},{2,6},{6,2},{1... | collective-permute-start | bytes 393224 | tf_op jit(solution)/shard_map/ppermute | solution.py:11
  73.3 5.4 %collective-permute-start.4 = (bf16[128,256]{1,0:T(8,128)(2,1)S(1)}, bf16[128,256]{1,0:T(8,128)(2,1)S(1)}, u32[]{:S(2)}, u32[]{:S(2)}) collective-permute-start(bf16[128,256]{1,0:T(8,128)(2,1)S(1)} %add.7), channel_id=1, source_target_pairs={{0,8},{4,12},{8,0},{12,4},{1,9},{5,13},{9,1},{13,5},{2,10},{6,14},... | collective-permute-start | bytes 196616 | tf_op jit(solution)/shard_map/ppermute | solution.py:11
  79.5 4.3 %collective-permute-start.5 = (bf16[128,256]{1,0:T(8,128)(2,1)S(1)}, bf16[128,256]{1,0:T(8,128)(2,1)S(1)}, u32[]{:S(2)}, u32[]{:S(2)}) collective-permute-start(bf16[128,256]{1,0:T(8,128)(2,1)S(1)} %fusion.7), channel_id=1, source_target_pairs={{0,4},{4,0},{8,12},{12,8},{1,5},{5,1},{9,13},{13,9},{2,6},{6,2},{1... | collective-permute-start | bytes 196616 | tf_op jit(solution)/shard_map/ppermute | solution.py:11
